TPU v7x, 256 devices: a whole 4x4x8 slice. The times are simulated.
256 devices in a mesh: ctx: 64 (over z_lo, x, y), rep: 4 (over z_hi, core).
Axes of the slice: x: 4, y: 4, z: 8 (z_hi: 2, z_lo: 4; z = z_hi * 4 + z_lo), core: 2. Of those that a mesh axis runs over, the one named last changes fastest.
Arguments:
- inputs: bfloat16 [4, 16384, 256], P('rep', 'ctx'), may hold values from -6 to 6
- w_expand: bfloat16 [512, 1024], replicated, may hold values from -0.25 to 0.25
- b_expand: float32 [1024], replicated, may hold values from -1 to 1
- w_reduce: bfloat16 [1024, 512], replicated, may hold values from -0.1875 to 0.1875
- b_reduce: float32 [512], replicated, may hold values from -0.5 to 0.5
- gate_logit: float32 [512], replicated, may hold values from -2 to 2
- cotangent: bfloat16 [4, 16384, 256], P('rep', 'ctx'), may hold values from -6 to 6
Outputs:
- outputs: bfloat16 [4, 16384, 256], P('rep', 'ctx')
- grad_inputs: bfloat16 [4, 16384, 256], P('rep', 'ctx')
- grad_w_expand: float32 [512, 1024], P('ctx')
- grad_b_expand: float32 [1024], replicated
- grad_w_reduce: float32 [1024, 512], P('ctx')
- grad_b_reduce: float32 [512], replicated
- grad_gate: float32 [512], replicated
All inputs are finite; a program needn't handle non-finite values.
Results may differ from a plain program's by a relative error of at most 0.018.
Values may be sent and summed in bfloat16 or wider, within the bound.
A program may use at most 64 MiB of HBM per device.

v0:
```python
import math
import jax
import jax.numpy as jnp
from jax import lax
from jax.sharding import PartitionSpec as P

SECTIONS = 4
EPSILON = 1e-05


def partner_2(value, axis, stride):
    mask = 2**stride
    pairs = [(source, source ^ mask) for source in range(lax.axis_size(axis))]
    return lax.ppermute(value, axis, pairs)


def gelu_back(preact, upstream):
    return jax.vjp(lambda value: jax.nn.gelu(value, approximate=False), preact)[1](upstream)[0]


def switch_forward(lower, upper, w_expand, b_expand):
    joined = jnp.concatenate([lower, upper], axis=-1).astype(jnp.float32)
    centred = joined - jnp.mean(joined, axis=-1, keepdims=True)
    inv_std = lax.rsqrt(jnp.mean(centred * centred, axis=-1, keepdims=True) + EPSILON)
    normed = centred * inv_std
    normed_low = normed.astype(jnp.bfloat16)
    preact = jnp.dot(normed_low, w_expand, preferred_element_type=jnp.float32) + b_expand
    hidden = jax.nn.gelu(preact, approximate=False).astype(jnp.bfloat16)
    return (joined, normed, inv_std, normed_low, preact, hidden)


def switch_apply(lower, upper, w_expand, b_expand, w_reduce, b_reduce, gate_logit):
    joined, normed, inv_std, normed_low, preact, hidden = switch_forward(
        lower, upper, w_expand, b_expand
    )
    mixed = jnp.dot(hidden, w_reduce, preferred_element_type=jnp.float32)
    result = (jax.nn.sigmoid(gate_logit) * joined + mixed + b_reduce).astype(jnp.bfloat16)
    width = lower.shape[-1]
    return (result[:, :width], result[:, width:])


def switch_backward(
    lower, upper, grad_lower, grad_upper, w_expand, b_expand, w_reduce, b_reduce, gate_logit
):
    joined, normed, inv_std, normed_low, preact, hidden = switch_forward(
        lower, upper, w_expand, b_expand
    )
    grad_out = jnp.concatenate([grad_lower, grad_upper], axis=-1)
    grad_float = grad_out.astype(jnp.float32)
    sigma = jax.nn.sigmoid(gate_logit)
    grad_bias_red = jnp.sum(grad_float, axis=0)
    grad_gate = jnp.sum(grad_float * joined, axis=0) * sigma * (1.0 - sigma)
    grad_weight_red = jnp.dot(hidden.T, grad_out, preferred_element_type=jnp.float32)
    grad_hidden = jnp.dot(grad_out, w_reduce.T, preferred_element_type=jnp.float32)
    grad_pre = gelu_back(preact, grad_hidden)
    grad_pre_low = grad_pre.astype(jnp.bfloat16)
    grad_bias_exp = jnp.sum(grad_pre, axis=0)
    grad_weight_exp = jnp.dot(normed_low.T, grad_pre_low, preferred_element_type=jnp.float32)
    grad_normed = jnp.dot(grad_pre_low, w_expand.T, preferred_element_type=jnp.float32)
    grad_joined = sigma * grad_float + inv_std * (
        grad_normed
        - jnp.mean(grad_normed, axis=-1, keepdims=True)
        - normed * jnp.mean(grad_normed * normed, axis=-1, keepdims=True)
    )
    grad_joined = grad_joined.astype(jnp.bfloat16)
    width = lower.shape[-1]
    return (
        grad_joined[:, :width],
        grad_joined[:, width:],
        (grad_weight_exp, grad_bias_exp, grad_weight_red, grad_bias_red, grad_gate),
    )


def body(inputs, w_expand, b_expand, w_reduce, b_reduce, gate_logit, cotangent):
    weights = (w_expand, b_expand, w_reduce, b_reduce, gate_logit)
    rows = inputs.shape[1]
    width = inputs.shape[2]
    devs = lax.axis_size("ctx")
    count = devs.bit_length() - 1
    position = lax.axis_index("ctx")
    totals = (
        jnp.zeros(w_expand.shape, jnp.float32),
        jnp.zeros(b_expand.shape, jnp.float32),
        jnp.zeros(w_reduce.shape, jnp.float32),
        jnp.zeros(b_reduce.shape, jnp.float32),
        jnp.zeros(gate_logit.shape, jnp.float32),
    )
    state = inputs.reshape(rows, width)
    saved = []
    for section in range(SECTIONS):
        bit = (count - 1 - section) % count
        upper_side = position >> bit & 1 == 1
        partner = partner_2(state, "ctx", bit)
        lower = jnp.where(upper_side, partner, state)
        upper = jnp.where(upper_side, state, partner)
        out_lower, out_upper = switch_apply(lower, upper, *weights)
        state = jnp.where(upper_side, out_upper, out_lower)
        saved.append((lower, upper, upper_side, bit))
    outputs = state.reshape(inputs.shape)
    grad_state = cotangent.reshape(rows, width)
    for section in reversed(range(SECTIONS)):
        lower, upper, upper_side, bit = saved[section]
        partner_grad = partner_2(grad_state, "ctx", bit)
        grad_lower = jnp.where(upper_side, partner_grad, grad_state)
        grad_upper = jnp.where(upper_side, grad_state, partner_grad)
        back_lower, back_upper, grads = switch_backward(
            lower, upper, grad_lower, grad_upper, *weights
        )
        grad_state = jnp.where(upper_side, back_upper, back_lower)
        totals = tuple((total + piece for total, piece in zip(totals, grads)))
    grad_inputs = grad_state.reshape(inputs.shape)
    share = 0.5
    factor = share / math.sqrt(lax.axis_size("rep") * devs * rows)
    part_expand, part_reduce = (
        lax.psum_scatter(totals[0], "ctx", scatter_dimension=0, tiled=True),
        lax.psum_scatter(totals[2], "ctx", scatter_dimension=0, tiled=True),
    )
    part_expand, part_reduce = (
        lax.psum(part_expand.astype(jnp.bfloat16), "rep").astype(jnp.float32),
        lax.psum(part_reduce.astype(jnp.bfloat16), "rep").astype(jnp.float32),
    )
    bias_expand, bias_reduce, gate_sum = lax.psum((totals[1], totals[3], totals[4]), ("ctx", "rep"))
    return (
        outputs,
        grad_inputs,
        part_expand * factor,
        bias_expand * factor,
        part_reduce * factor,
        bias_reduce * factor,
        gate_sum * factor,
    )


def solution(mesh):
    return jax.shard_map(
        body,
        mesh=mesh,
        in_specs=(P("rep", "ctx", None), P(), P(), P(), P(), P(), P("rep", "ctx", None)),
        out_specs=(
            P("rep", "ctx", None),
            P("rep", "ctx", None),
            P("ctx", None),
            P(),
            P("ctx", None),
            P(),
            P(),
        ),
        check_vma=False,
    )
```

profile of v0, /device:TPU:1, one launch (start us, length us, event | category | flops | bytes accessed | tf_op | source)
XLA Modules:
  0.0 865.5 jit_solution(2419286555103033543)
XLA Ops:
  7.2 3.9 collective-permute-start
  11.1 0.7 add_divide_fusion
  11.8 1.9 collective-permute-done
  13.7 0.9 broadcast_select_fusion.3
  14.8 0.2 fusion.67
  15.0 4.6 multiply_convert_fusion.3
  19.6 0.4 fusion.70
  20.1 5.0 collective-permute-start.1
  25.1 2.4 collective-permute-done.1
  27.6 0.2 fusion.61
  27.9 3.8 multiply_convert_fusion.2
  31.6 0.8 copy-done.1
  32.4 0.4 fusion.74
  32.9 3.0 collective-permute-start.2
  35.9 0.3 collective-permute-start.4
  36.2 2.1 collective-permute-done.2
  38.5 0.2 fusion.55
  38.7 2.6 multiply_convert_fusion.1
  41.3 0.4 fusion.78
  41.8 1.6 collective-permute-start.3
  43.4 2.4 collective-permute-done.3
  46.3 2.6 multiply_convert_fusion
  48.9 0.7 fusion.127
  49.6 0.6 fusion.120
  50.3 1.2 fusion.48
  51.5 3.0 collective-permute-start.5
  54.5 0.6 fusion.95
  55.1 1.9 collective-permute-done.5
  57.0 0.7 fusion.128
  57.7 0.6 fusion.119
  58.3 0.2 fusion.54
  58.6 2.3 collective-permute-start.6
  60.9 0.6 fusion.91
  61.5 1.8 collective-permute-done.6
  63.3 0.7 fusion.126
  64.1 0.6 fusion.118
  64.7 0.2 fusion.60
  65.0 3.4 collective-permute-start.7
  68.4 0.6 fusion.87
  69.0 2.7 collective-permute-done.7
  71.8 0.7 fusion.125
  72.5 2.0 add_add_fusion.1
  74.5 0.3 reduce-scatter.5.cloned.1.call-start
  74.8 1.6 fusion.115
  76.4 0.5 fusion.113
  76.8 0.6 copy-done.2
  77.4 0.5 fusion.111
  77.9 1.8 add_add_fusion
  79.7 0.9 copy-done.6
  80.6 0.7 fusion.100
  81.3 0.7 fusion.117
  82.0 87.2 %all-reduce = (f32[1024]{0:T(1024)S(1)}, f32[512]{0:T(512)S(1)}, f32[512]{0:T(512)S(1)}) all-reduce(f32[1024]{0:T(1024)S(1)} %add_add_fusion.2, f32[512]{0:T(512)S(1)} %get-tuple-element.71, f32[512]{0:T(512)S(1)} %get-tuple-element.70), channel_id=1, replica_groups=mesh['ctx'=64,'rep'=4] {'ctx','rep'}, use_global_device_ids=true, to_apply=%region_22.23 | all-reduce | flops 2048 | bytes 16384 | tf_op jit(solution)/shard_map/psum | solution.py:122
  169.2 0.6 broadcast_multiply_fusion.2
  169.8 0.6 broadcast_multiply_fusion.1
  170.4 0.6 broadcast_multiply_fusion
  171.0 0.2 fusion.66
  171.2 0.7 fusion.99
  171.9 240.2 %reduce-scatter.3.cloned.1.call-done = f32[8,1024]{1,0:T(8,128)} async-done(((f32[512,1024]{1,0:T(8,128)}), f32[8,1024]{1,0:T(8,128)}) %reduce-scatter.3.cloned.1.call-update) | async-done | bytes 32784 | tf_op jit(solution)/shard_map/reduce_scatter | solution.py:115
  412.1 0.8 convert_element_type.136
  412.8 373.4 %reduce-scatter.5.cloned.1.call-done = f32[16,512]{1,0:T(8,128)} async-done(((f32[1024,512]{1,0:T(8,128)}), f32[16,512]{1,0:T(8,128)}) %reduce-scatter.5.cloned.1.call-update) | async-done | bytes 32784 | tf_op jit(solution)/shard_map/reduce_scatter | solution.py:116
  786.2 0.8 convert_element_type.138
  787.0 70.5 %all-reduce.1 = (bf16[8,1024]{1,0:T(8,128)(2,1)S(1)}, bf16[16,512]{1,0:T(8,128)(2,1)S(1)}) all-reduce(bf16[8,1024]{1,0:T(8,128)(2,1)S(1)} %convert_element_type.136, bf16[16,512]{1,0:T(8,128)(2,1)S(1)} %convert_element_type.138), channel_id=1, replica_groups=mesh['ctx'=64,'rep'=4] {'rep'}, use_global_device_ids=true, to_apply=%region_17.18 | all-reduce | flops 16384 | bytes 65536 | tf_op jit(solution)/shard_map/psum | solution.py:119
  857.5 0.6 convert_multiply_fusion.13
  858.1 0.6 convert_multiply_fusion.12
  (72 shorter events, 1.2 us)
Async XLA Ops:
  7.2 7.8 copy-start
  7.2 404.9 %reduce-scatter.3.cloned.1.call-start = ((), (), s32[]{:S(2)}) async-start(), calls=%async_computation.2 | async-start | bytes 2129920 | tf_op jit(solution)/shard_map/reduce_scatter | solution.py:115
  7.2 6.5 collective-permute-start
  15.0 4.6 copy-start.9
  15.0 4.6 copy-start.13
  19.6 8.3 copy-start.12
  20.1 7.4 collective-permute-start.1
  27.9 4.6 copy-start.10
  31.6 0.8 copy-start.1
  31.6 4.2 copy-start.7
  32.9 5.4 collective-permute-start.2
  35.9 7.5 collective-permute-start.4
  38.7 2.6 copy-start.11
  41.3 4.7 copy-start.3
  41.8 4.1 collective-permute-start.3
  48.9 1.4 copy-start.5
  51.5 5.4 collective-permute-start.5
  58.6 4.7 copy-start.16
  58.6 4.7 copy-start.17
  58.6 4.7 collective-permute-start.6
  65.0 6.8 copy-start.14
  65.0 6.8 copy-start.15
  65.0 6.7 collective-permute-start.7
  74.5 711.7 %reduce-scatter.5.cloned.1.call-start = ((), (), s32[]{:S(2)}) async-start(), calls=%async_computation.3 | async-start | bytes 2129920 | tf_op jit(solution)/shard_map/reduce_scatter | solution.py:116
  74.8 1.6 copy-start.4
  76.4 1.0 copy-start.2
  79.7 0.9 copy-start.6
  79.7 2.3 copy-start.8
Sparse Core Ops, SparseCore 0:
  74.6 337.3 reduce-scatter.2
  414.5 371.6 reduce-scatter.4
where the time goes:
time: 866 us
  waiting for transfers between devices  629 us (73%)
  blocking collectives  158 us (18%)
  matrix products  29.5 us (3%)
  starting transfers between devices  22.8 us (3%)
  between operations  14.5 us (2%)
  other arithmetic  9.87 us (1%)
    reduce_scatter x1, waiting for transfers between devices, body(): lax.psum_scatter(totals[2], 'ctx', scatter_dimension=0, tiled=True)  373 us
    reduce_scatter x1, waiting for transfers between devices, body(): lax.psum_scatter(totals[0], 'ctx', scatter_dimension=0, tiled=True)  240 us
    psum x1, blocking collectives, body(): lax.psum((totals[1], totals[3], totals[4]), ('ctx', 'rep'))  87.2 us
    psum x1, blocking collectives, body(): lax.psum(part_expand.astype(jnp.bfloat16), 'rep').astype(jnp.float32)  70.5 us
    ppermute x8, starting transfers between devices, partner_2(): return lax.ppermute(value, axis, pairs)  22.5 us
  transfers between devices with their start and end apart: 10, of which 9 were waited for; matrix products, arithmetic and copies ran while one was open for 2% of the time, Pallas kernels for 0%

commit v1 on v0

--- a/solution.py
+++ b/solution.py
@@ -119,7 +119,9 @@
         lax.psum(part_expand.astype(jnp.bfloat16), "rep").astype(jnp.float32),
         lax.psum(part_reduce.astype(jnp.bfloat16), "rep").astype(jnp.float32),
     )
-    bias_expand, bias_reduce, gate_sum = lax.psum((totals[1], totals[3], totals[4]), ("ctx", "rep"))
+    bias_expand, bias_reduce, gate_sum = lax.psum(
+        lax.psum((totals[1], totals[3], totals[4]), "ctx"), "rep"
+    )
     return (
         outputs,
         grad_inputs,

time: 866 us -> 865 us (level)
  waiting for transfers between devices: 629 us -> 506 us
  blocking collectives: 158 us -> 279 us
    psum x1 -> x2, blocking collectives: 87.2 us -> 209 us  [the longest x1 166 us: body(): lax.psum((totals[1], totals[3], totals[4]), 'ctx')]
    reduce_scatter x1, waiting for transfers between devices: 240 us -> 120 us  [body(): lax.psum_scatter(totals[0], 'ctx', scatter_dimension=0, tiled=True)]
where the time goes in v1:
time: 865 us
  waiting for transfers between devices  506 us (58%)
  blocking collectives  279 us (32%)
  matrix products  29.5 us (3%)
  starting transfers between devices  22.8 us (3%)
  between operations  14.6 us (2%)
  other arithmetic  9.88 us (1%)
    reduce_scatter x1, waiting for transfers between devices, body(): lax.psum_scatter(totals[2], 'ctx', scatter_dimension=0, tiled=True)  371 us
    psum x1, blocking collectives, body(): lax.psum((totals[1], totals[3], totals[4]), 'ctx')  166 us
    reduce_scatter x1, waiting for transfers between devices, body(): lax.psum_scatter(totals[0], 'ctx', scatter_dimension=0, tiled=True)  120 us
    psum x1, blocking collectives, body(): lax.psum(part_expand.astype(jnp.bfloat16), 'rep').astype(jnp.float32)  69.8 us
    psum x1, blocking collectives, body(): lax.psum(lax.psum((totals[1], totals[3], totals[4]), 'ctx'), 'rep')  43.7 us
    ppermute x8, starting transfers between devices, partner_2(): return lax.ppermute(value, axis, pairs)  22.5 us
  transfers between devices with their start and end apart: 10, of which 9 were waited for; matrix products, arithmetic and copies ran while one was open for 2% of the time, Pallas kernels for 0%

profile of v1, /device:TPU:1, one launch (start us, length us, event | category | flops | bytes accessed | tf_op | source)
XLA Modules:
  0.0 864.7 jit_solution(13033708270511414089)
XLA Ops:
  7.2 3.9 collective-permute-start
  11.1 0.7 add_divide_fusion
  11.8 1.9 collective-permute-done
  13.7 0.9 broadcast_select_fusion.3
  14.8 0.2 fusion.67
  15.0 4.6 multiply_convert_fusion.3
  19.6 0.4 fusion.70
  20.1 5.0 collective-permute-start.1
  25.1 2.4 collective-permute-done.1
  27.9 3.8 multiply_convert_fusion.2
  31.6 0.8 copy-done.1
  32.4 0.4 fusion.74
  32.9 3.0 collective-permute-start.2
  35.9 0.3 collective-permute-start.4
  36.2 2.1 collective-permute-done.2
  38.5 0.2 fusion.55
  38.7 2.6 multiply_convert_fusion.1
  41.3 0.5 fusion.78
  41.8 1.6 collective-permute-start.3
  43.5 2.4 collective-permute-done.3
  46.3 2.6 multiply_convert_fusion
  48.9 0.7 fusion.127
  49.6 0.6 fusion.120
  50.2 1.2 fusion.48
  51.5 3.0 collective-permute-start.5
  54.5 0.6 fusion.95
  55.1 1.8 collective-permute-done.5
  56.9 0.7 fusion.128
  57.7 0.6 fusion.119
  58.3 0.2 fusion.54
  58.6 2.3 collective-permute-start.6
  60.9 0.6 fusion.91
  61.5 1.8 collective-permute-done.6
  63.3 0.7 fusion.126
  64.0 0.6 fusion.118
  64.7 0.2 fusion.60
  65.0 3.4 collective-permute-start.7
  68.3 0.6 fusion.87
  68.9 2.7 collective-permute-done.7
  71.7 0.7 fusion.125
  72.4 2.0 add_add_fusion.1
  74.4 0.3 reduce-scatter.5.cloned.1.call-start
  74.7 1.6 fusion.115
  76.3 0.5 fusion.113
  76.8 0.6 copy-done.2
  77.3 0.5 fusion.111
  77.8 1.8 add_add_fusion
  79.6 0.9 copy-done.6
  80.6 0.7 fusion.100
  81.2 0.7 fusion.117
  81.9 165.6 %all-reduce = (f32[1024]{0:T(1024)S(1)}, f32[512]{0:T(512)S(1)}, f32[512]{0:T(512)S(1)}) all-reduce(f32[1024]{0:T(1024)S(1)} %add_add_fusion.2, f32[512]{0:T(512)S(1)} %get-tuple-element.74, f32[512]{0:T(512)S(1)} %get-tuple-element.73), channel_id=1, replica_groups=mesh['ctx'=64,'rep'=4] {'ctx'}, use_global_device_ids=true, to_apply=%region_22.23 | all-reduce | flops 2048 | bytes 16384 | tf_op jit(solution)/shard_map/psum | solution.py:123
  247.6 43.7 %all-reduce.1 = (f32[1024]{0:T(1024)S(1)}, f32[512]{0:T(512)S(1)}, f32[512]{0:T(512)S(1)}) all-reduce(f32[1024]{0:T(1024)S(1)} %get-tuple-element.23, f32[512]{0:T(512)S(1)} %get-tuple-element.24, f32[512]{0:T(512)S(1)} %get-tuple-element.25), channel_id=1, replica_groups=mesh['ctx'=64,'rep'=4] {'rep'}, use_global_device_ids=true, to_apply=%region_23.24 | all-reduce | flops 2048 | bytes 16384 | tf_op jit(solution)/shard_map/psum | solution.py:122
  291.3 0.6 broadcast_multiply_fusion.2
  291.9 0.6 broadcast_multiply_fusion.1
  292.5 0.6 broadcast_multiply_fusion
  293.1 0.2 fusion.66
  293.3 0.7 fusion.99
  294.0 120.0 %reduce-scatter.3.cloned.1.call-done = f32[8,1024]{1,0:T(8,128)} async-done(((f32[512,1024]{1,0:T(8,128)}), f32[8,1024]{1,0:T(8,128)}) %reduce-scatter.3.cloned.1.call-update) | async-done | bytes 32784 | tf_op jit(solution)/shard_map/reduce_scatter | solution.py:115
  413.9 0.8 convert_element_type.136
  414.7 371.3 %reduce-scatter.5.cloned.1.call-done = f32[16,512]{1,0:T(8,128)} async-done(((f32[1024,512]{1,0:T(8,128)}), f32[16,512]{1,0:T(8,128)}) %reduce-scatter.5.cloned.1.call-update) | async-done | bytes 32784 | tf_op jit(solution)/shard_map/reduce_scatter | solution.py:116
  786.0 0.8 convert_element_type.138
  786.8 69.8 %all-reduce.2 = (bf16[8,1024]{1,0:T(8,128)(2,1)S(1)}, bf16[16,512]{1,0:T(8,128)(2,1)S(1)}) all-reduce(bf16[8,1024]{1,0:T(8,128)(2,1)S(1)} %convert_element_type.136, bf16[16,512]{1,0:T(8,128)(2,1)S(1)} %convert_element_type.138), channel_id=1, replica_groups=mesh['ctx'=64,'rep'=4] {'rep'}, use_global_device_ids=true, to_apply=%region_17.18 | all-reduce | flops 16384 | bytes 65536 | tf_op jit(solution)/shard_map/psum | solution.py:119
  856.6 0.6 convert_multiply_fusion.13
  857.2 0.6 convert_multiply_fusion.12
  (73 shorter events, 1.4 us)
Async XLA Ops:
  7.2 7.8 copy-start
  7.2 406.7 %reduce-scatter.3.cloned.1.call-start = ((), (), s32[]{:S(2)}) async-start(), calls=%async_computation.2 | async-start | bytes 2129920 | tf_op jit(solution)/shard_map/reduce_scatter | solution.py:115
  7.2 6.5 collective-permute-start
  15.0 4.6 copy-start.9
  15.0 4.6 copy-start.13
  19.6 8.3 copy-start.12
  20.1 7.4 collective-permute-start.1
  27.9 4.6 copy-start.10
  31.6 0.8 copy-start.1
  31.6 4.2 copy-start.7
  32.9 5.4 collective-permute-start.2
  35.9 7.5 collective-permute-start.4
  38.7 2.6 copy-start.11
  41.3 4.7 copy-start.3
  41.8 4.1 collective-permute-start.3
  48.9 1.4 copy-start.5
  51.5 5.4 collective-permute-start.5
  58.6 4.7 copy-start.16
  58.6 4.7 copy-start.17
  58.6 4.6 collective-permute-start.6
  64.9 6.8 copy-start.14
  64.9 6.8 copy-start.15
  65.0 6.7 collective-permute-start.7
  74.4 711.6 %reduce-scatter.5.cloned.1.call-start = ((), (), s32[]{:S(2)}) async-start(), calls=%async_computation.3 | async-start | bytes 2129920 | tf_op jit(solution)/shard_map/reduce_scatter | solution.py:116
  74.7 1.6 copy-start.4
  76.3 1.0 copy-start.2
  79.6 0.9 copy-start.6
  79.6 2.3 copy-start.8
Sparse Core Ops, SparseCore 0:
  74.6 339.3 reduce-scatter.2
  416.4 369.5 reduce-scatter.4
